TPU v7x, 32 devices: a whole 2x2x4 slice. The times are simulated.
32 devices in a mesh: dp: 1, seq: 32 (over z, y, x, core).
Axes of the slice: x: 2, y: 2, z: 4, core: 2. Of those that a mesh axis runs over, the one named last changes fastest.
Arguments:
- waveform: float32 [1, 163840], P('dp', 'seq'), may hold values from -45 to 45
- lengths: int32 [1, 4], P('dp'), may hold values from 1 to 30, 60 in all within a row
- conv_first: float32 [10, 512], replicated, may hold values from -2 to 2
- conv_second: bfloat16 [1536, 512], replicated, may hold values from -0.15625 to 0.15625
- cotangent: bfloat16 [1, 16384, 512], P('dp', 'seq'), may hold values from -6 to 6
Outputs:
- features: bfloat16 [1, 16384, 512], P('dp', 'seq')
- grad_first: float32 [10, 512], replicated
- grad_second: float32 [1536, 512], replicated
All inputs are finite; a program needn't handle non-finite values.
Results may differ from a plain program's by a relative error of at most 0.001.
The roundings to bfloat16 on the way count: a program that leaves them out, or rounds other values in their place, can miss the bound.
Values sent between devices are 32-bit elements; how exact they have to be, the bound alone decides.
A program may use at most 64 MiB of HBM per device.

v0:
```python
import jax
import jax.numpy as jnp
from jax import lax
from jax.sharding import PartitionSpec as P

MIN_UNITS = 50


HIGH = lax.Precision.HIGHEST


def from_behind(x, axis, by):
    count = lax.axis_size(axis)
    pairs = [(i, i + by) for i in range(count) if 0 <= i + by < count]
    return lax.ppermute(x, axis, pairs)


def gelu_exact(value):
    return 0.5 * value * (1.0 + lax.erf(value * 0.7071067811865476))


def gelu_slope(value):
    return (
        0.5 * (1.0 + lax.erf(value * 0.7071067811865476))
        + value * jnp.exp(-0.5 * value * value) * 0.3989422804014327
    )


def frame_info(lengths_row, first_sample, frame_count, stride):
    utt_units = lengths_row + (MIN_UNITS - 1)
    utt_ends = jnp.cumsum(utt_units, dtype=jnp.int32) * 640
    starts = utt_ends - utt_units * 640
    places = first_sample + stride * jnp.arange(frame_count, dtype=jnp.int32)
    inside = (places[:, None] >= starts[None, :]) & (places[:, None] < utt_ends[None, :])
    end_of = jnp.sum(jnp.where(inside, utt_ends[None, :], 0), axis=1, dtype=jnp.int32)
    counts = (utt_units * 128 - 1).astype(jnp.float32)
    return (inside.astype(jnp.float32), places, end_of, counts)


def first_layer(extended, conv_first, frame_count):
    blocks = extended.reshape(frame_count + 1, 5)
    patches = jnp.concatenate([blocks[:-1], blocks[1:]], axis=1)
    return (
        patches,
        jnp.dot(patches, conv_first, precision=HIGH, preferred_element_type=jnp.float32),
    )


def second_rows(first_out, frame_count):
    pairs = first_out[:frame_count].reshape(frame_count // 2, 2 * first_out.shape[1])
    third = first_out[2 : frame_count + 1 : 2]
    return jnp.concatenate([pairs, third], axis=1)


def spread_back(slopes, frame_count, channels):
    near_part = slopes[:, : 2 * channels].reshape(frame_count, channels)
    far_part = slopes[:, 2 * channels :]
    spread = jnp.stack([far_part, jnp.zeros_like(far_part)], axis=1).reshape(frame_count, channels)
    padded = jnp.concatenate([jnp.zeros((2, channels), slopes.dtype), spread], axis=0)
    return (near_part + padded[:frame_count], padded[frame_count : frame_count + 1])


def on_device(waveform, lengths, conv_first, conv_second, cotangent):
    seq_size = lax.axis_size("seq")
    seq_index = lax.axis_index("seq")
    samples = waveform[0]
    lengths_row = lengths[0]
    frame_count = samples.shape[0] // 5
    out_count = frame_count // 2
    channels = conv_second.shape[1]
    first_sample = seq_index * samples.shape[0]
    ahead = from_behind(samples[:10], "seq", -1)
    extended = jnp.concatenate([samples, ahead])
    patches, first_pre = first_layer(extended, conv_first, frame_count + 1)
    member, places, end_of, counts = frame_info(lengths_row, first_sample, frame_count + 1, 5)
    first_valid = (places + 10 <= end_of).astype(jnp.float32)[:, None]
    own_member = member[:frame_count]
    own_pre = first_pre[:frame_count] * first_valid[:frame_count]
    part_one = jnp.dot(own_member.T, own_pre, precision=HIGH)
    part_two = jnp.dot(own_member.T, own_pre * first_pre[:frame_count], precision=HIGH)
    sum_one, sum_two = lax.psum((part_one, part_two), "seq")
    utt_mean = sum_one / counts[:, None]
    utt_var = sum_two / counts[:, None] - utt_mean * utt_mean
    utt_rstd = lax.rsqrt(utt_var + 1e-05)
    frame_mean = jnp.dot(member, utt_mean, precision=HIGH)
    frame_rstd = jnp.dot(member, utt_rstd, precision=HIGH)
    first_norm = (first_pre - frame_mean) * frame_rstd
    first_out = (gelu_exact(first_norm) * first_valid).astype(jnp.bfloat16)
    rows_second = second_rows(first_out, frame_count)
    second_pre = jnp.dot(rows_second, conv_second, preferred_element_type=jnp.float32)
    out_member, out_places, out_end, out_counts = frame_info(
        lengths_row, first_sample, out_count, 10
    )
    second_valid = (out_places + 20 <= out_end).astype(jnp.float32)[:, None]
    features = (gelu_exact(second_pre) * second_valid).astype(jnp.bfloat16)
    second_delta = (
        cotangent[0].astype(jnp.float32) * second_valid * gelu_slope(second_pre)
    ).astype(jnp.bfloat16)
    grad_second = jnp.dot(rows_second.T, second_delta, preferred_element_type=jnp.float32)
    slopes = jnp.dot(second_delta, conv_second.T, preferred_element_type=jnp.float32)
    first_delta, outgoing = spread_back(slopes, frame_count, channels)
    incoming = from_behind(outgoing, "seq", 1)
    first_delta = first_delta + jnp.concatenate(
        [incoming, jnp.zeros((frame_count - 1, channels), jnp.float32)], axis=0
    )
    own_valid = first_valid[:frame_count]
    own_norm = first_norm[:frame_count]
    norm_delta = first_delta * gelu_slope(own_norm) * own_valid
    part_back_one = jnp.dot(own_member.T, norm_delta, precision=HIGH)
    part_back_two = jnp.dot(own_member.T, norm_delta * own_norm, precision=HIGH)
    back_one, back_two = lax.psum((part_back_one, part_back_two), "seq")
    back_one = back_one / counts[:, None]
    back_two = back_two / counts[:, None]
    pre_delta = (
        frame_rstd[:frame_count]
        * own_valid
        * (
            norm_delta
            - jnp.dot(own_member, back_one, precision=HIGH)
            - own_norm * jnp.dot(own_member, back_two, precision=HIGH)
        )
    )
    grad_first = jnp.dot(patches[:frame_count].T, pre_delta, precision=HIGH)
    factor = float(lax.axis_size("dp") * out_count * seq_size) ** (-0.5)
    total_second, total_first = lax.psum((grad_second, grad_first), ("dp", "seq"))
    return (features[None], total_first * factor, total_second * factor)


def solution(mesh):
    placed = (P("dp", "seq"), P("dp", None), P(), P(), P("dp", "seq", None))
    return jax.shard_map(
        on_device,
        mesh=mesh,
        in_specs=placed,
        out_specs=(P("dp", "seq", None), P(), P()),
        check_vma=False,
    )
```

profile of v0, /device:TPU:1, one launch (start us, length us, event | category | flops | bytes accessed | tf_op | source)
XLA Modules:
  0.0 245.5 jit_solution(7816088722351553091)
XLA Ops:
  8.0 2.0 collective-permute-start
  11.7 2.0 collective-permute-done
  15.8 1.9 fusion.36
  19.9 39.7 %all-reduce.4 = (f32[4,512]{1,0:T(4,128)S(1)}, f32[4,512]{1,0:T(4,128)S(1)}) all-reduce(f32[4,512]{1,0:T(4,128)S(1)} %fusion.7, f32[4,512]{1,0:T(4,128)S(1)} %fusion.1), channel_id=1, replica_groups=mesh['dp'=1,'seq'=32] {'seq'}, use_global_device_ids=true, to_apply=%region_3.4 | all-reduce | flops 4096 | bytes 32768 | tf_op jit(solution)/shard_map/psum | solution.py:81
  59.6 1.1 fusion.47
  61.2 3.1 %multiply_convert_fusion = (bf16[1025,512]{1,0:T(8,128)(2,1)S(1)}, f32[1025,512]{1,0:T(8,128)}) fusion(f32[1025]{0:T(1024)S(1)} %fusion.50, f32[1025,512]{1,0:T(8,128)S(1)} %fusion.47, f32[1025,512]{1,0:T(8,128)S(1)} %copy-done.2, pred[1025,4]{0,1:T(4,128)(4,1)S(1)} %get-tuple-element.8, f32[4,512]{1,0:T(4,128)S(1)} %get-tuple-element.6, ...), kind=kOutput, calls=%fused_computation.7 | convolution fusion | flops 29390848 | bytes 7363608 | tf_op jit(solution)/shard_map/dot_general | solution.py:85
  64.3 3.6 %slice.83 = bf16[512,512]{1,0:T(8,128)(2,1)} slice(bf16[1025,512]{1,0:T(8,128)(2,1)S(1)} %get-tuple-element.15), slice={[2:1025:2], [0:512:1]} | slice | bytes 1048576 | tf_op jit(solution)/shard_map/slice | solution.py:51
  69.0 1.4 reshape.106
  70.4 3.4 %fusion.29 = (bf16[512,512]{1,0:T(8,128)(2,1)S(1)}, bf16[1,512,512]{2,1,0:T(8,128)(2,1)}) fusion(bf16[1,512,512]{2,1,0:T(8,128)(2,1)} %param.9, f32[512]{0:T(512)S(1)} %fusion.55, bf16[1536,512]{1,0:T(8,128)(2,1)S(1)} %copy-done, bf16[512,512]{1,0:T(8,128)(2,1)} %slice.83, bf16[512,1024]{1,0:T(8,128)(2,1)S(1)} %reshape.106), kind=kOutput, calls=%fused_computation.37 | convolution fusion | flops 812646400 | bytes 4720640 | tf_op jit(solution)/shard_map/dot_general | solution.py:90
  74.9 1.7 copy-done.8
  76.6 1.1 copy.16
  77.7 2.1 stack.7.clone
  79.8 3.7 %reshape.108 = f32[1024,512]{1,0:T(8,128)} reshape(f32[512,2,512]{2,1,0:T(2,128)} %stack.7.clone) | data formatting | bytes 4194304 | tf_op jit(solution)/shard_map/reshape | solution.py:58
  84.2 5.4 %collective-permute-start.1 = (f32[1,512]{1,0:T(1,128)S(1)}, f32[1,512]{1,0:T(1,128)S(1)}, u32[]{:S(2)}, u32[]{:S(2)}) collective-permute-start(f32[1,512]{1,0:T(1,128)S(1)} %slice.100), channel_id=1, source_target_pairs={{0,1},{1,2},{2,3},{3,4},{4,5},{5,6},{6,7},{7,8},{8,9},{9,10},{10,1... | collective-permute-start | bytes 6152 | tf_op jit(solution)/shard_map/ppermute | solution.py:15
  89.6 3.7 %fusion.33 = f32[1536,512]{1,0:T(8,128)} fusion(bf16[512,512]{1,0:T(8,128)(2,1)S(1)} %get-tuple-element.9, bf16[512,512]{1,0:T(8,128)(2,1)} %slice.83, bf16[512,1024]{1,0:T(8,128)(2,1)S(1)} %reshape.106), kind=kOutput, calls=%fused_computation.45 | convolution fusion | flops 808452096 | bytes 5242880 | tf_op jit(solution)/shard_map/dot_general | solution.py:99
  93.3 3.2 %slice.98 = f32[512,1024]{1,0:T(8,128)} slice(f32[512,1536]{1,0:T(8,128)} %copy-done.8), slice={[0:512], [0:1024]} | slice | bytes 4194304 | tf_op jit(solution)/shard_map/slice | solution.py:56
  96.5 2.7 %reshape.107 = f32[1024,512]{1,0:T(8,128)} reshape(f32[512,1024]{1,0:T(8,128)} %slice.98) | data formatting | bytes 4194304 | tf_op jit(solution)/shard_map/reshape | solution.py:56
  99.3 3.9 %fusion.6 = f32[1024,512]{1,0:T(8,128)S(1)} fusion(f32[1024,512]{1,0:T(8,128)} %reshape.107, f32[1024,512]{1,0:T(8,128)} %reshape.108, f32[1,512]{1,0:T(1,128)S(1)} %collective-permute-done.1, f32[1025,512]{1,0:T(8,128)} %get-tuple-element.16, f32[1024]{0:T(1024)S(1)} %slice.95), kind=kLoop, calls=%fused_computation.11 | loop fusion | flops 6291456 | bytes 8394752 | tf_op jit(solution)/shard_map/mul | solution.py:108
  105.3 38.5 %all-reduce.3 = (f32[4,512]{1,0:T(4,128)S(1)}, f32[4,512]{1,0:T(4,128)S(1)}) all-reduce(f32[4,512]{1,0:T(4,128)S(1)} %fusion.17, f32[4,512]{1,0:T(4,128)S(1)} %fusion.66), channel_id=1, replica_groups=mesh['dp'=1,'seq'=32] {'seq'}, use_global_device_ids=true, to_apply=%region_6.7 | all-reduce | flops 4096 | bytes 32768 | tf_op jit(solution)/shard_map/psum | solution.py:111
  144.9 1.0 fusion.45
  146.1 3.2 %fusion.13 = f32[10,512]{1,0:T(8,128)S(1)} fusion(f32[1025,512]{1,0:T(8,128)} %copy-done.7, f32[1024,512]{1,0:T(8,128)S(1)} %fusion.43, f32[1024,512]{1,0:T(8,128)S(1)} %copy-done.4, f32[1024,512]{1,0:T(8,128)S(1)} %fusion.45, f32[1025,512]{1,0:T(8,128)S(1)} %copy-done.6, f32[1024]{0:T(1024)S(1)} %slice.95, f32[1025,5]{0,1:T(8,128)S(1)} %copy.14, ...), kind=kOutput, calls=%fused_computation.19 | convolution fusion | flops 65546240 | bytes 10584064 | tf_op jit(solution)/shard_map/dot_general | solution.py:123
  149.4 39.0 %psum.46 = f32[10,512]{1,0:T(8,128)S(1)} all-reduce(f32[10,512]{1,0:T(8,128)S(1)} %fusion.13), channel_id=1, replica_groups=mesh['dp'=1,'seq'=32] {'dp','seq'}, use_global_device_ids=true, to_apply=%region_7.8 | all-reduce | flops 5120 | bytes 40960 | tf_op jit(solution)/shard_map/psum | solution.py:125
  189.0 45.8 %all-reduce.7.cloned.1.call-done = f32[1536,512]{1,0:T(8,128)} async-done(((f32[1536,512]{1,0:T(8,128)}), f32[1536,512]{1,0:T(8,128)}) %all-reduce.7.cloned.1.call-update) | async-done | bytes 3145744 | tf_op jit(solution)/shard_map/psum | solution.py:125
  234.8 3.9 %broadcast_multiply_fusion = f32[1536,512]{1,0:T(8,128)} fusion(f32[1536,512]{1,0:T(8,128)} %all-reduce.7.cloned.1.call-done), kind=kLoop, calls=%fused_computation.30 | loop fusion | flops 786432 | bytes 6291456 | tf_op jit(solution)/shard_map/mul | solution.py:126
  (49 shorter events, 14.1 us)
Async XLA Ops:
  7.2 63.3 %copy-start = (bf16[1536,512]{1,0:T(8,128)(2,1)S(1)}, bf16[1536,512]{1,0:T(8,128)(2,1)}, u32[]{:S(2)}) copy-start(bf16[1536,512]{1,0:T(8,128)(2,1)} %param.8) | copy-start | bytes 4718596
  7.2 8.6 %copy-start.9 = (f32[10,512]{1,0:T(8,128)S(1)}, f32[10,512]{1,0:T(8,128)}, u32[]{:S(2)}) copy-start(f32[10,512]{1,0:T(8,128)} %param.7) | copy-start | bytes 61444
  7.2 227.6 %all-reduce.7.cloned.1.call-start = ((), (), s32[]{:S(2)}) async-start(), calls=%async_computation | async-start | bytes 6291456 | tf_op jit(solution)/shard_map/psum | solution.py:125
  8.0 5.7 %collective-permute-start = (f32[10]{0:T(128)S(1)}, f32[10]{0:T(128)S(1)}, u32[]{:S(2)}, u32[]{:S(2)}) collective-permute-start(f32[10]{0:T(128)S(1)} %slice_bitcast_fusion.1), channel_id=1, source_target_pairs={{1,0},{2,1},{3,2},{4,3},{5,4},{6,5},{7,6},{8,7},{9,8},{10,9},{11,1... | collective-permute-start | bytes 128 | tf_op jit(solution)/shard_map/ppermute | solution.py:15
  17.7 1.3 copy-start.1
  59.6 1.6 copy-start.2
  61.2 3.1 %copy-start.7 = (f32[1025,512]{1,0:T(8,128)}, f32[1025,512]{1,0:T(8,128)S(1)}, u32[]{:S(2)}) copy-start(f32[1025,512]{1,0:T(8,128)S(1)} %fusion.47) | copy-start | bytes 6297604
  74.9 1.7 copy-start.8
  84.2 15.1 %collective-permute-start.1 = (f32[1,512]{1,0:T(1,128)S(1)}, f32[1,512]{1,0:T(1,128)S(1)}, u32[]{:S(2)}, u32[]{:S(2)}) collective-permute-start(f32[1,512]{1,0:T(1,128)S(1)} %slice.100), channel_id=1, source_target_pairs={{0,1},{1,2},{2,3},{3,4},{4,5},{5,6},{6,7},{7,8},{8,9},{9,10},{10,1... | collective-permute-start | bytes 6152 | tf_op jit(solution)/shard_map/ppermute | solution.py:15
  99.2 4.0 %copy-start.5 = (f32[1025,512]{1,0:T(8,128)S(1)}, f32[1025,512]{1,0:T(8,128)}, u32[]{:S(2)}) copy-start(f32[1025,512]{1,0:T(8,128)} %get-tuple-element.16) | copy-start | bytes 6297604
  103.2 1.3 copy-start.3
  143.8 2.1 copy-start.4
  143.8 2.3 copy-start.6
Sparse Core Ops, SparseCore 0:
  99.4 135.3 all-reduce.6
where the time goes:
time: 248 us; the launch traced here: 246 us
  blocking collectives  117 us (47%)
  waiting for transfers between devices  47.8 us (19%)
  local copies, waits for them, and re-layouts  24.7 us (10%)
  matrix products  23.1 us (9%)
  between operations  14.3 us (6%)
  other arithmetic  11.1 us (4%)
  starting transfers between devices  7.39 us (3%)
    psum x1, waiting for transfers between devices, on_device(): lax.psum((grad_second, grad_first), ('dp', 'seq'))  45.8 us
    psum x1, blocking collectives, on_device(): sum_one, sum_two = lax.psum((part_one, part_two), 'seq')  39.7 us
    psum x1, blocking collectives, on_device(): lax.psum((grad_second, grad_first), ('dp', 'seq'))  39 us
    psum x1, blocking collectives, on_device(): back_one, back_two = lax.psum((part_back_one, part_back_two), 'seq')  38.5 us
    ppermute x2, starting transfers between devices, from_behind(): return lax.ppermute(x, axis, pairs)  7.35 us
  transfers between devices with their start and end apart: 3, of which 2 were waited for; matrix products, arithmetic and copies ran while one was open for 9% of the time, Pallas kernels for 0%

commit v1 on v0

v1 whole, which is shorter than its diff:
```python
import functools

import jax
import jax.numpy as jnp
from jax import lax
from jax.experimental import pallas as pl
from jax.experimental.pallas import tpu as pltpu
from jax.sharding import PartitionSpec as P

MIN_UNITS = 50
TAPS = 10
HIGH = lax.Precision.HIGHEST
MESH = pl.DeviceIdType.MESH
F32 = jnp.float32
BLOCK = 64


def dot_tn(a, b, precision=None):
    return lax.dot_general(
        a, b, (((0,), (0,)), ((), ())), precision=precision, preferred_element_type=F32
    )


def dot_nt(a, b):
    return lax.dot_general(a, b, (((1,), (1,)), ((), ())), preferred_element_type=F32)


def stage_orders(bits):
    if bits != 5:
        return [list(range(bits))] * 4
    return [[0, 1, 2, 3, 4], [0, 2, 3, 1, 4], [0, 3, 1, 2, 4], [0, 1, 2, 3, 4]]


class Part:
    def __init__(self, me, order, src, inbox, out, size, send_sems, recv_sems):
        self.me, self.order, self.src, self.inbox, self.out = me, order, src, inbox, out
        self.send_sems, self.recv_sems = send_sems, recv_sems
        self.stages = len(order)
        self.size, self.off, self.room, self.at = size, 0, 0, 0
        self.copies = []

    def bit(self, stage):
        return (self.me // (1 << self.order[stage])) % 2

    def send(self, src, dst, stage, number):
        partner = self.me + (1 - 2 * self.bit(stage)) * (1 << self.order[stage])
        copy = pltpu.make_async_remote_copy(
            src_ref=src,
            dst_ref=dst,
            send_sem=self.send_sems.at[number],
            recv_sem=self.recv_sems.at[number],
            device_id={"seq": partner},
            device_id_type=MESH,
        )
        copy.start()
        self.copies.append(copy)

    def start(self):
        if self.at < self.stages:
            half = self.size // 2
            bit = self.bit(self.at)
            self.send(
                self.src.at[pl.ds(self.off + (1 - bit) * half, half)],
                self.inbox.at[pl.ds(self.room, half)],
                self.at,
                self.at,
            )
            self.off = self.off + bit * half
            self.size = half
        elif self.at < 2 * self.stages:
            own = self.out.at[pl.ds(self.off, self.size)]
            self.send(own, own, 2 * self.stages - 1 - self.at, self.at)

    def finish(self):
        self.copies[self.at].wait_recv()
        if self.at < self.stages:
            last = self.at == self.stages - 1
            target = self.out if last else self.src
            step = min(self.size, 16)

            def add(i, carry):
                here = pl.ds(self.off + i * step, step)
                target[here] = self.src[here] + self.inbox[pl.ds(self.room + i * step, step)]
                return carry

            lax.fori_loop(0, self.size // step, add, 0)
            self.room += self.size
        else:
            bit = self.bit(2 * self.stages - 1 - self.at)
            self.off = self.off - bit * self.size
            self.size = self.size * 2
        self.at += 1

    def step(self):
        self.finish()
        self.start()

    def drain(self):
        for copy in self.copies:
            copy.wait_send()


def kernel(
    n, factor,
    lengths_ref, taps_ref, first_ref, second_ref, cot_ref,
    feat_ref, grad1_ref, grad2_ref,
    norm_ref, slope_ref, q_ref, x_ref, sd_ref,
    slots_a, slots_b, buf, inbox, outb, ex, ex_in, ex_out, erow,
    send_sems, recv_sems, stat_send, stat_recv,
):
    me = lax.axis_index("seq")
    rows = sd_ref.shape[0]
    channels = first_ref.shape[1]
    utts = lengths_ref.shape[1]
    bits = n.bit_length() - 1
    low = min(3, bits)
    group = 1 << low
    groups = n // group
    my_low, my_high = me % group, me // group
    first_sample = me * (rows * TAPS)

    barrier = pltpu.get_barrier_semaphore()
    orders = stage_orders(bits)

    def flip(mask):
        out = me
        for b in range(bits):
            if mask >> b & 1:
                out = out + (1 - 2 * ((me // (1 << b)) % 2)) * (1 << b)
        return out

    stat_masks = list(range(1, group)) + [k * group for k in range(1, groups)]
    all_masks = sorted(set(stat_masks) | {1 << b for b in range(bits)})
    for mask in all_masks:
        pl.semaphore_signal(
            barrier, inc=1, device_id={"seq": flip(mask)}, device_id_type=MESH
        )

    units = [lengths_ref[0, u] + (MIN_UNITS - 1) for u in range(utts)]
    ends, total = [], jnp.int32(0)
    for u in range(utts):
        total = total + units[u] * 640
        ends.append(total)
    here = jnp.int32(0)
    for u in range(utts - 1):
        here = here + jnp.where(first_sample >= ends[u], 1, 0)
    end_a, end_b = jnp.int32(0), jnp.int32(0)
    for u in range(utts):
        end_a = jnp.where(here == u, ends[u], end_a)
        end_b = jnp.where(here + 1 == u, ends[u], end_b)

    def masks(t, start, count, width):
        row = lax.broadcasted_iota(jnp.int32, (count, width), 0) + start
        place = first_sample + 5 * t + TAPS * row
        is_b = place >= end_a
        valid = place + TAPS <= jnp.where(is_b, end_b, end_a)
        return is_b, valid

    lane = lax.broadcasted_iota(jnp.int32, (BLOCK, 128), 1)
    lane_b = ((lane >= 16) & (lane < 32)) | (lane == 33)

    zero_row = jnp.zeros((1, channels), F32)
    sq = (zero_row, zero_row)
    for t in range(3):
        def conv_block(i, carry, t=t):
            start = pl.multiple_of(i * BLOCK, BLOCK)
            at = pl.ds(pl.multiple_of(t * rows + i * BLOCK, BLOCK), BLOCK)
            taps = taps_ref[at]
            pre = jnp.dot(taps, first_ref[...], precision=HIGH, preferred_element_type=F32)
            norm_ref[at] = pre
            is_b, valid = masks(t, start, BLOCK, 128)
            q_ref[at] = jnp.where(valid & (is_b == lane_b), taps, 0.0)
            if t == 2:
                return carry
            is_b, valid = masks(t, start, BLOCK, channels)
            square = jnp.where(valid, pre * pre, 0.0)
            in_b = jnp.where(is_b, square, 0.0)
            in_a = jnp.where(is_b, 0.0, square)
            return (
                carry[0] + jnp.sum(in_a, axis=0, keepdims=True),
                carry[1] + jnp.sum(in_b, axis=0, keepdims=True),
            )

        sq = lax.fori_loop(0, rows // BLOCK, conv_block, sq)
    both = pl.ds(0, 2 * rows)
    sums = dot_tn(q_ref[both], norm_ref[both], HIGH)

    def spread(a, b):
        return [
            jnp.where(here == u, a, jnp.where(here + 1 == u, b, jnp.zeros_like(a)))
            for u in range(utts)
        ]

    stats = spread(sums[32:33], sums[33:34]) + spread(sq[0], sq[1])
    slots_a[my_low] = jnp.concatenate(stats, axis=0)
    pl.semaphore_wait(barrier, len(all_masks))

    def exchange(slots, mine, members, number):
        copies = []
        for i, mask in enumerate(members):
            copy = pltpu.make_async_remote_copy(
                src_ref=slots.at[mine],
                dst_ref=slots.at[mine],
                send_sem=stat_send.at[number + i],
                recv_sem=stat_recv.at[number + i],
                device_id={"seq": flip(mask)},
                device_id_type=MESH,
            )
            copy.start()
            copies.append(copy)
        return copies

    stat_copies = exchange(slots_a, my_low, range(1, group), 0)
    qq = dot_tn(q_ref[both], q_ref[both], HIGH)
    for copy in stat_copies:
        copy.wait_recv()
    total = slots_a[0]
    for i in range(1, group):
        total = total + slots_a[i]
    if groups > 1:
        slots_b[my_high] = total
        more = exchange(slots_b, my_high, [k * group for k in range(1, groups)], group - 1)
        for copy in more:
            copy.wait_recv()
        stat_copies = stat_copies + more
        total = slots_b[0]
        for i in range(1, groups):
            total = total + slots_b[i]
    means, rstds, inverse = [], [], []
    for u in range(utts):
        count = jnp.full((1, channels), units[u] * 128 - 1, jnp.int32).astype(F32)
        mean = total[u : u + 1] / count
        var = total[utts + u : utts + u + 1] / count - mean * mean
        means.append(mean)
        rstds.append(lax.rsqrt(var + 1e-05))
        inverse.append(count)

    def pick(values, offset):
        out = zero_row
        for u in range(utts):
            out = jnp.where(here + offset == u, values[u], out)
        return out

    mean_a, mean_b = pick(means, 0), pick(means, 1)
    rstd_a, rstd_b = pick(rstds, 0), pick(rstds, 1)

    for t in range(3):
        def gelu_block(i, carry, t=t):
            start = pl.multiple_of(i * 32, 32)
            at = pl.ds(pl.multiple_of(t * rows + i * 32, 32), 32)
            is_b, valid = masks(t, start, 32, channels)
            norm = (norm_ref[at] - jnp.where(is_b, mean_b, mean_a)) * jnp.where(
                is_b, rstd_b, rstd_a
            )
            norm_ref[at] = norm
            cdf = 0.5 * (1.0 + lax.erf(norm * 0.7071067811865476))
            x_ref[at] = jnp.where(valid, norm * cdf, 0.0).astype(jnp.bfloat16)
            slope = cdf + norm * jnp.exp(-0.5 * norm * norm) * 0.3989422804014327
            slope_ref[at] = jnp.where(valid, slope, 0.0)
            return carry

        lax.fori_loop(0, rows // 32, gelu_block, 0)

    def second_block(i, carry):
        start = pl.multiple_of(i * 128, 128)
        pre = jnp.zeros((128, channels), F32)
        for t in range(3):
            pre = pre + jnp.dot(
                x_ref[pl.ds(pl.multiple_of(t * rows + i * 128, 128), 128)],
                second_ref[t * channels : (t + 1) * channels],
                preferred_element_type=F32,
            )
        row = lax.broadcasted_iota(jnp.int32, (128, channels), 0) + start
        place = first_sample + TAPS * row
        valid = place + 2 * TAPS <= jnp.where(place >= end_a, end_b, end_a)
        cdf = 0.5 * (1.0 + lax.erf(pre * 0.7071067811865476))
        at = pl.ds(start, 128)
        feat_ref[at] = jnp.where(valid, pre * cdf, 0.0).astype(jnp.bfloat16)
        slope = cdf + pre * jnp.exp(-0.5 * pre * pre) * 0.3989422804014327
        sd_ref[at] = jnp.where(valid, cot_ref[at].astype(F32) * slope, 0.0).astype(jnp.bfloat16)
        return carry

    lax.fori_loop(0, rows // 128, second_block, 0)

    blocks = channels // 128
    tall = channels // 8
    size = blocks * tall
    parts = []
    for t in range(3):
        part = Part(
            me, orders[t], buf.at[pl.ds(t * size, size)], inbox.at[pl.ds(t * size, size)],
            outb.at[pl.ds(t * size, size)], size, send_sems.at[t], recv_sems.at[t],
        )
        grad = dot_tn(x_ref[t * rows : (t + 1) * rows], sd_ref[...])
        for c in range(blocks):
            buf[t * size + c * tall : t * size + (c + 1) * tall] = grad[
                :, c * 128 : (c + 1) * 128
            ].reshape(tall, 8, 128)
        part.start()
        parts.append(part)

    back = (zero_row, zero_row, zero_row, zero_row)
    for t in range(3):
        weight = second_ref.at[t * channels : (t + 1) * channels]

        def back_block(i, carry, t=t, weight=weight):
            start = pl.multiple_of(i * BLOCK, BLOCK)
            at = pl.ds(pl.multiple_of(t * rows + i * BLOCK, BLOCK), BLOCK)
            delta = dot_nt(sd_ref[pl.ds(start, BLOCK)], weight[...]) * slope_ref[at]
            slope_ref[at] = delta
            is_b, _ = masks(t, start, BLOCK, channels)
            scaled = delta * norm_ref[at]
            add = [jnp.where(is_b, 0.0, delta), jnp.where(is_b, delta, 0.0)]
            add += [jnp.where(is_b, 0.0, scaled), jnp.where(is_b, scaled, 0.0)]
            return tuple(c + jnp.sum(a, axis=0, keepdims=True) for c, a in zip(carry, add))

        back = lax.fori_loop(0, rows // BLOCK, back_block, back)
    for part in parts:
        part.step()
    acc = dot_tn(q_ref[...], slope_ref[...], HIGH)

    grad_a = rstd_a * acc[0:16] + rstd_b * acc[16:32]
    erow[0:16] = grad_a
    one = spread(back[0], back[1])
    two = spread(back[2], back[3])
    erow[16:24] = jnp.concatenate(one + two, axis=0)
    norm_a = rstd_a * (sums[0:16] - qq[0:16, 32:33] * mean_a)
    norm_b = rstd_b * (sums[16:32] - qq[16:32, 33:34] * mean_b)
    per = spread(norm_a, norm_b)
    for u in range(utts):
        erow[24 + u * TAPS : 24 + (u + 1) * TAPS] = per[u][:TAPS]
    for u, w in enumerate(spread(qq[32:33], qq[33:34])):
        erow[10 + u : 11 + u, 0:128] = w
    high = erow.shape[0] // 8
    for c in range(blocks):
        ex[c * high : (c + 1) * high] = erow[:, c * 128 : (c + 1) * 128].reshape(high, 8, 128)
    extra = Part(
        me, orders[3], ex, ex_in, ex_out, blocks * high, send_sems.at[3], recv_sems.at[3]
    )
    extra.start()
    for _ in range(2 * bits - 1):
        for part in parts:
            part.step()
        extra.step()
    extra.finish()
    for t in range(3):
        for c in range(blocks):
            grad2_ref[t * channels : (t + 1) * channels, c * 128 : (c + 1) * 128] = (
                outb[t * size + c * tall : t * size + (c + 1) * tall].reshape(channels, 128) * factor
            )
    for c in range(blocks):
        erow[:, c * 128 : (c + 1) * 128] = ex_out[c * high : (c + 1) * high].reshape(8 * high, 128)
    weights, scales = [], []
    result = erow[0:TAPS]
    for u in range(utts):
        weights.append(erow[10 + u : 11 + u, 0:128])
        scales.append(rstds[u] * (erow[16 + u : 17 + u] / inverse[u]))
        result = result - rstds[u] * (erow[16 + utts + u : 17 + utts + u] / inverse[u]) * (
            erow[24 + u * TAPS : 24 + (u + 1) * TAPS]
        )
    pad = [jnp.zeros((8 - utts, 128), F32)], [jnp.zeros((8 - utts, channels), F32)]
    plain = dot_tn(
        jnp.concatenate(weights + pad[0], axis=0), jnp.concatenate(scales + pad[1], axis=0), HIGH
    )
    grad1_ref[...] = (result - plain[0:TAPS] - plain[16 : 16 + TAPS]) * factor
    for copy in stat_copies:
        copy.wait_send()
    for part in parts + [extra]:
        part.drain()


def on_device(waveform, lengths, conv_first, conv_second, cotangent):
    n = lax.axis_size("seq")
    samples = waveform[0]
    rows = samples.shape[0] // TAPS
    channels = conv_second.shape[1]
    utts = lengths.shape[1]
    assert 24 + utts * TAPS <= 64 and utts == 4 and samples.shape[0] < MIN_UNITS * 640
    ahead = lax.ppermute(samples[:TAPS], "seq", [(i, i - 1) for i in range(1, n)])
    table = jnp.concatenate([samples, ahead]).reshape(rows + 1, TAPS)
    middle = jnp.concatenate([table[:-1, 5:], table[1:, :5]], axis=1)
    taps = jnp.concatenate([table[:-1], middle, table[1:]], axis=0)
    count = 3 * rows
    gap = jnp.zeros((count, 6), F32)
    taps = jnp.concatenate(
        [taps, gap, taps, gap, jnp.ones((count, 2), F32), jnp.zeros((count, 94), F32)], axis=1
    )
    first = jnp.concatenate([conv_first, jnp.zeros((128 - TAPS, channels), F32)], axis=0)
    factor = float(lax.axis_size("dp") * rows * n) ** (-0.5)
    tiles = 3 * channels // 8 * (channels // 128)
    small = 64 // 8 * (channels // 128)
    bits = n.bit_length() - 1
    vmem = pl.BlockSpec(memory_space=pltpu.VMEM)
    feats, grad1, grad2 = pl.pallas_call(
        functools.partial(kernel, n, factor),
        name="encoder",
        out_shape=(
            jax.ShapeDtypeStruct((rows, channels), jnp.bfloat16),
            jax.ShapeDtypeStruct((TAPS, channels), F32),
            jax.ShapeDtypeStruct((3 * channels, channels), F32),
        ),
        in_specs=[pl.BlockSpec(memory_space=pltpu.SMEM)] + [vmem] * 4,
        out_specs=(vmem, vmem, vmem),
        scratch_shapes=[
            pltpu.VMEM((count, channels), F32),
            pltpu.VMEM((count, channels), F32),
            pltpu.VMEM((count, 128), F32),
            pltpu.VMEM((count, channels), jnp.bfloat16),
            pltpu.VMEM((rows, channels), jnp.bfloat16),
            pltpu.VMEM((8, 2 * utts, channels), F32),
            pltpu.VMEM((max(1, n // 8), 2 * utts, channels), F32),
            pltpu.VMEM((tiles, 8, 128), F32),
            pltpu.VMEM((tiles, 8, 128), F32),
            pltpu.VMEM((tiles, 8, 128), F32),
            pltpu.VMEM((small, 8, 128), F32),
            pltpu.VMEM((small, 8, 128), F32),
            pltpu.VMEM((small, 8, 128), F32),
            pltpu.VMEM((64, channels), F32),
            pltpu.SemaphoreType.DMA((4, 2 * bits)),
            pltpu.SemaphoreType.DMA((4, 2 * bits)),
            pltpu.SemaphoreType.DMA((8 + n // 8,)),
            pltpu.SemaphoreType.DMA((8 + n // 8,)),
        ],
        compiler_params=pltpu.CompilerParams(
            collective_id=0, has_side_effects=True, vmem_limit_bytes=60 * 1024 * 1024
        ),
    )(lengths, taps, first, conv_second, cotangent[0])
    if lax.axis_size("dp") > 1:
        grad1, grad2 = lax.psum((grad1, grad2), "dp")
    return (feats[None], grad1, grad2)


def solution(mesh):
    placed = (P("dp", "seq"), P("dp", None), P(), P(), P("dp", "seq", None))
    return jax.shard_map(
        on_device,
        mesh=mesh,
        in_specs=placed,
        out_specs=(P("dp", "seq", None), P(), P()),
        check_vma=False,
    )
```

time: 248 us -> 100 us (0.40)
  blocking collectives: 117 us -> 0 us
  Pallas kernels: 0 us -> 80.6 us
  waiting for transfers between devices: 47.8 us -> 0.11 us
  matrix products: 23.1 us -> 0 us
  between operations: 14.3 us -> 0.71 us
  local copies, waits for them, and re-layouts: 24.7 us -> 13.1 us
  other arithmetic: 11.1 us -> 3.1 us
  starting transfers between devices: 7.39 us -> 1.95 us
    psum x3 -> x0, blocking collectives: 117 us -> none  [the longest x1 39.7 us: on_device(): sum_one, sum_two = lax.psum((part_one, part_two), 'seq')]
    pallas_call x0 -> x1, Pallas kernels: none -> 80.6 us  [on_device(): pl.pallas_call(functools.partial(kernel, n, factor), name='encoder', out_...]
    psum x1 -> x0, waiting for transfers between devices: 45.8 us -> none  [on_device(): lax.psum((grad_second, grad_first), ('dp', 'seq'))]
    dot_general x13 -> x0, matrix products: 23.1 us -> none  [the longest x1 3.72 us: on_device(): jnp.dot(rows_second.T, second_delta, preferred_element_type=jnp.float32)]
    slice x10 -> x4, local copies, waits for them, and re-layouts: 10.5 us -> 1.22 us  [the longest x1 0.66 us: on_device(): samples[:TAPS]]
    mul x4 -> x0, other arithmetic: 8.48 us -> none  [the longest x2 4.54 us: on_device(): return (features[None], total_first * factor, total_second * factor)]
    reshape x3 -> x1, local copies, waits for them, and re-layouts: 7.79 us -> 0.21 us  [on_device(): table = jnp.concatenate([samples, ahead]).reshape(rows + 1, TAPS)]
    ppermute x2 -> x1, starting transfers between devices: 7.35 us -> 1.95 us  [on_device(): lax.ppermute(samples[:TAPS], 'seq', [(i, i - 1) for i in range(1, n)])]
  transfers between devices with their start and end apart: 3 -> 1, of which waited for: 2 -> 1; matrix products, arithmetic and copies ran while one was open for 9% -> 4% of each run, Pallas kernels for 0% -> 0%
where the time goes in v1:
time: 100 us; the launch traced here: 99.6 us
  Pallas kernels  80.6 us (81%)
  local copies, waits for them, and re-layouts  13.1 us (13%)
  other arithmetic  3.1 us (3%)
  starting transfers between devices  1.95 us (2%)
    pallas_call x1, Pallas kernels, on_device(): pl.pallas_call(functools.partial(kernel, n, factor), name='encoder', out_...  80.6 us
    unnamed x4, local copies, waits for them, and re-layouts  7.61 us
    concatenate x1, local copies, waits for them, and re-layouts, on_device(): jnp.concatenate([taps, gap, taps, gap, jnp.ones((count, 2), F32), jnp.zer...  2.44 us
  transfers between devices with their start and end apart: 1, of which 1 were waited for; matrix products, arithmetic and copies ran while one was open for 4% of the time, Pallas kernels for 0%

profile of v1, /device:TPU:1, one launch (start us, length us, event | category | flops | bytes accessed | tf_op | source)
XLA Modules:
  0.0 99.6 jit_solution(14969155145325848432)
XLA Ops:
  0.6 0.7 slice_bitcast_fusion
  1.3 2.0 %collective-permute-start = (f32[10]{0:T(128)S(1)}, f32[10]{0:T(128)S(1)}, u32[]{:S(2)}, u32[]{:S(2)}) collective-permute-start(f32[10]{0:T(128)S(1)} %slice_bitcast_fusion), channel_id=1, source_target_pairs={{1,0},{2,1},{3,2},{4,3},{5,4},{6,5},{7,6},{8,7},{9,8},{10,9},{11,1... | collective-permute-start | bytes 128 | tf_op jit(solution)/shard_map/ppermute | solution.py:379
  3.2 0.5 broadcast.5
  3.8 1.4 %reduce.3 = f32[5120]{0:T(1024)S(1)} reduce(f32[1,5120]{1,0:T(1,128)} %param.5, f32[]{:T(128)} %broadcast.5), dimensions={0}, to_apply=%param.5.reduce_sub_computation.3 | reduce | bytes 40964 | tf_op args[0]
  5.2 0.2 slice.32
  5.4 1.5 %concatenate.19.first_ref = f32[128,512]{1,0:T(8,128)} pad(f32[10,512]{1,0:T(8,128)} %param.7, f32[]{:T(128)} %constant.2.clone.1), padding=0_118x0_0 | pad | bytes 282628 | tf_op jit(solution)/shard_map/concatenate | solution.py:388
  6.9 0.1 collective-permute-done
  7.0 0.7 pad_maximum_fusion.1
  7.7 0.2 reshape.23
  8.0 0.8 fusion
  8.8 0.2 slice.38
  9.0 0.1 fusion.1
  9.1 0.1 pad_maximum_fusion
  9.3 0.1 broadcast_in_dim.15
  9.3 0.1 broadcast_in_dim.13
  9.4 0.1 broadcast_in_dim.14
  9.4 2.4 %concatenate.18.taps_ref = f32[1536,128]{1,0:T(8,128)} concatenate(f32[1536,10]{1,0:T(8,128)S(1)} %pad_maximum_fusion, f32[1536,6]{1,0:T(8,128)S(1)} %broadcast_in_dim.13, f32[1536,10]{1,0:T(8,128)S(1)} %pad_maximum_fusion, f32[1536,6]{1,0:T(8,128)S(1)} %broadcast_in_dim.13, f32[1536,2]{1,0:T(8,128)S(1)} %broadcast_in_dim.14, f32[1536,94]{1,0:T(8,128)S(1)} %broadcast_in_dim.15), dimensions={1} | concatenate | bytes 1572864 | tf_op jit(solution)/shard_map/concatenate | solution.py:385
  11.9 80.6 %encoder.1 = (bf16[512,512]{1,0:T(8,128)(2,1)}, f32[10,512]{1,0:T(8,128)}, f32[1536,512]{1,0:T(8,128)}) custom-call(s32[1,4]{1,0:T(1,128)} %lengths_ref.1, f32[1536,128]{1,0:T(8,128)} %concatenate.18.taps_ref, f32[128,512]{1,0:T(8,128)} %concatenate.19.first_ref, bf16[1536,512]{1,0:T(8,128)(2,1)} %second_ref.1, bf16[512,512]{1,0:T(8,128)(2,1)} %bitcast.6), custom_call_target="tpu_custom_call" | custom-call | tf_op jit(solution)/shard_map/encoder/pallas_call | solution.py:394
  92.5 1.9 %copy.20 = bf16[1,512,512]{2,1,0:T(8,128)(2,1)} copy(bf16[1,512,512]{2,1,0:T(8,128)(2,1)} %bitcast.5) | data formatting | bytes 1048576
  94.4 1.4 %copy.21 = f32[10,512]{1,0:T(8,128)} copy(f32[10,512]{1,0:T(8,128)} %get-tuple-element.15) | data formatting | bytes 40960
  95.8 3.9 %copy.22 = f32[1536,512]{1,0:T(8,128)} copy(f32[1536,512]{1,0:T(8,128)} %get-tuple-element.16) | data formatting | bytes 6291456
Async XLA Ops:
  1.3 5.7 %collective-permute-start = (f32[10]{0:T(128)S(1)}, f32[10]{0:T(128)S(1)}, u32[]{:S(2)}, u32[]{:S(2)}) collective-permute-start(f32[10]{0:T(128)S(1)} %slice_bitcast_fusion), channel_id=1, source_target_pairs={{1,0},{2,1},{3,2},{4,3},{5,4},{6,5},{7,6},{8,7},{9,8},{10,9},{11,1... | collective-permute-start | bytes 128 | tf_op jit(solution)/shard_map/ppermute | solution.py:379

commit v2 on v1

--- a/solution.py
+++ b/solution.py
@@ -102,15 +102,16 @@
 
 def kernel(
     n, factor,
-    lengths_ref, taps_ref, first_ref, second_ref, cot_ref,
-    feat_ref, grad1_ref, grad2_ref,
+    lengths_ref, wave_ref, conv_ref, second_ref, cot_ref,
+    feat_ref, grad1_ref, outb,
+    tab_ref, halo_ref, taps_ref, first_ref,
     norm_ref, slope_ref, q_ref, x_ref, sd_ref,
-    slots_a, slots_b, buf, inbox, outb, ex, ex_in, ex_out, erow,
-    send_sems, recv_sems, stat_send, stat_recv,
+    slots_a, slots_b, buf, inbox, ex, ex_in, ex_out, erow,
+    send_sems, recv_sems, stat_send, stat_recv, halo_sems,
 ):
     me = lax.axis_index("seq")
     rows = sd_ref.shape[0]
-    channels = first_ref.shape[1]
+    channels = conv_ref.shape[1]
     utts = lengths_ref.shape[1]
     bits = n.bit_length() - 1
     low = min(3, bits)
@@ -135,6 +136,24 @@
         pl.semaphore_signal(
             barrier, inc=1, device_id={"seq": flip(mask)}, device_id_type=MESH
         )
+    pl.semaphore_signal(
+        barrier, inc=1, device_id={"seq": lax.rem(me + 1, n)}, device_id_type=MESH
+    )
+    tab_ref[...] = jnp.zeros_like(tab_ref)
+    tab_ref[0:rows, 0:TAPS] = wave_ref[...]
+    first_ref[...] = jnp.zeros_like(first_ref)
+    for t in range(3):
+        first_ref[t * 128 + 5 * t : t * 128 + 5 * t + TAPS] = conv_ref[...]
+    pl.semaphore_wait(barrier, len(all_masks) + 1)
+    halo = pltpu.make_async_remote_copy(
+        src_ref=tab_ref.at[pl.ds(0, 8)],
+        dst_ref=halo_ref,
+        send_sem=halo_sems.at[0],
+        recv_sem=halo_sems.at[1],
+        device_id={"seq": lax.rem(me + n - 1, n)},
+        device_id_type=MESH,
+    )
+    halo.start()
 
     units = [lengths_ref[0, u] + (MIN_UNITS - 1) for u in range(utts)]
     ends, total = [], jnp.int32(0)
@@ -157,19 +176,26 @@
         return is_b, valid
 
     lane = lax.broadcasted_iota(jnp.int32, (BLOCK, 128), 1)
-    lane_b = ((lane >= 16) & (lane < 32)) | (lane == 33)
+    lane_b = ((lane >= 32) & (lane < 64)) | (lane == 65)
 
     zero_row = jnp.zeros((1, channels), F32)
     sq = (zero_row, zero_row)
     for t in range(3):
+        if t == 1:
+            halo.wait_recv()
+            tab_ref[rows : rows + 8] = jnp.where(me == n - 1, 0.0, halo_ref[...])
+            own = tab_ref[0:rows] + pltpu.roll(tab_ref[1 : rows + 1], TAPS, 1)
+            wide = lax.broadcasted_iota(jnp.int32, (rows, 128), 1)
+            ones = jnp.where((wide == 64) | (wide == 65), 1.0, 0.0)
+            taps_ref[...] = own + pltpu.roll(own, 32, 1) + ones
+
         def conv_block(i, carry, t=t):
             start = pl.multiple_of(i * BLOCK, BLOCK)
             at = pl.ds(pl.multiple_of(t * rows + i * BLOCK, BLOCK), BLOCK)
-            taps = taps_ref[at]
-            pre = jnp.dot(taps, first_ref[...], precision=HIGH, preferred_element_type=F32)
+            taps = (taps_ref if t else tab_ref)[pl.ds(start, BLOCK)]
+            weight = first_ref[t * 128 : (t + 1) * 128]
+            pre = jnp.dot(taps, weight, precision=HIGH, preferred_element_type=F32)
             norm_ref[at] = pre
-            is_b, valid = masks(t, start, BLOCK, 128)
-            q_ref[at] = jnp.where(valid & (is_b == lane_b), taps, 0.0)
             if t == 2:
                 return carry
             is_b, valid = masks(t, start, BLOCK, channels)
@@ -182,8 +208,25 @@
             )
 
         sq = lax.fori_loop(0, rows // BLOCK, conv_block, sq)
-    both = pl.ds(0, 2 * rows)
-    sums = dot_tn(q_ref[both], norm_ref[both], HIGH)
+
+    def taps_block(i, carry):
+        start = pl.multiple_of(i * BLOCK, BLOCK)
+        taps = taps_ref[pl.ds(start, BLOCK)]
+        for t in range(3):
+            is_b, valid = masks(t, start, BLOCK, 128)
+            at = pl.ds(pl.multiple_of(t * rows + i * BLOCK, BLOCK), BLOCK)
+            q_ref[at] = jnp.where(valid & (is_b == lane_b), taps, 0.0)
+        return carry
+
+    lax.fori_loop(0, rows // BLOCK, taps_block, 0)
+
+    def by_tap(ref, t):
+        return dot_tn(q_ref[t * rows : (t + 1) * rows], ref[t * rows : (t + 1) * rows], HIGH)
+
+    sums = [by_tap(norm_ref, t) for t in range(2)]
+    pre_a = sums[0][0:TAPS] + sums[1][5 : 5 + TAPS]
+    pre_b = sums[0][32 : 32 + TAPS] + sums[1][37 : 37 + TAPS]
+    one_ab = sums[0][64:72] + sums[1][64:72]
 
     def spread(a, b):
         return [
@@ -191,9 +234,8 @@
             for u in range(utts)
         ]
 
-    stats = spread(sums[32:33], sums[33:34]) + spread(sq[0], sq[1])
+    stats = spread(one_ab[0:1], one_ab[1:2]) + spread(sq[0], sq[1])
     slots_a[my_low] = jnp.concatenate(stats, axis=0)
-    pl.semaphore_wait(barrier, len(all_masks))
 
     def exchange(slots, mine, members, number):
         copies = []
@@ -210,8 +252,11 @@
             copies.append(copy)
         return copies
 
-    stat_copies = exchange(slots_a, my_low, range(1, group), 0)
-    qq = dot_tn(q_ref[both], q_ref[both], HIGH)
+    stat_copies = exchange(slots_a, my_low, range(group - 1, 0, -1), 0)
+    qq = [by_tap(q_ref, t) for t in range(2)]
+    w_rows = qq[0][64:72] + pltpu.roll(qq[1][64:72], 123, 1)
+    w_a = qq[0][0:TAPS, 64:65] + qq[1][5 : 5 + TAPS, 64:65]
+    w_b = qq[0][32 : 32 + TAPS, 65:66] + qq[1][37 : 37 + TAPS, 65:66]
     for copy in stat_copies:
         copy.wait_recv()
     total = slots_a[0]
@@ -219,21 +264,21 @@
         total = total + slots_a[i]
     if groups > 1:
         slots_b[my_high] = total
-        more = exchange(slots_b, my_high, [k * group for k in range(1, groups)], group - 1)
+        more = exchange(slots_b, my_high, [k * group for k in range(groups - 1, 0, -1)], group - 1)
         for copy in more:
             copy.wait_recv()
         stat_copies = stat_copies + more
         total = slots_b[0]
         for i in range(1, groups):
             total = total + slots_b[i]
-    means, rstds, inverse = [], [], []
+    means, rstds, counts = [], [], []
     for u in range(utts):
         count = jnp.full((1, channels), units[u] * 128 - 1, jnp.int32).astype(F32)
         mean = total[u : u + 1] / count
         var = total[utts + u : utts + u + 1] / count - mean * mean
         means.append(mean)
         rstds.append(lax.rsqrt(var + 1e-05))
-        inverse.append(count)
+        counts.append(count)
 
     def pick(values, offset):
         out = zero_row
@@ -301,13 +346,15 @@
 
     back = (zero_row, zero_row, zero_row, zero_row)
     for t in range(3):
-        weight = second_ref.at[t * channels : (t + 1) * channels]
-
-        def back_block(i, carry, t=t, weight=weight):
+        here_t = pl.ds(t * rows, rows)
+        slope_ref[here_t] = slope_ref[here_t] * dot_nt(
+            sd_ref[...], second_ref[t * channels : (t + 1) * channels]
+        )
+
+        def back_block(i, carry, t=t):
             start = pl.multiple_of(i * BLOCK, BLOCK)
             at = pl.ds(pl.multiple_of(t * rows + i * BLOCK, BLOCK), BLOCK)
-            delta = dot_nt(sd_ref[pl.ds(start, BLOCK)], weight[...]) * slope_ref[at]
-            slope_ref[at] = delta
+            delta = slope_ref[at]
             is_b, _ = masks(t, start, BLOCK, channels)
             scaled = delta * norm_ref[at]
             add = [jnp.where(is_b, 0.0, delta), jnp.where(is_b, delta, 0.0)]
@@ -315,21 +362,24 @@
             return tuple(c + jnp.sum(a, axis=0, keepdims=True) for c, a in zip(carry, add))
 
         back = lax.fori_loop(0, rows // BLOCK, back_block, back)
-    for part in parts:
-        part.step()
-    acc = dot_tn(q_ref[...], slope_ref[...], HIGH)
-
-    grad_a = rstd_a * acc[0:16] + rstd_b * acc[16:32]
-    erow[0:16] = grad_a
+        for part in parts:
+            part.step()
+    acc = [by_tap(slope_ref, t) for t in range(3)]
+
+    grad_a = jnp.zeros((TAPS, channels), F32)
+    for t in range(3):
+        grad_a = grad_a + rstd_a * acc[t][5 * t : 5 * t + TAPS]
+        grad_a = grad_a + rstd_b * acc[t][32 + 5 * t : 32 + 5 * t + TAPS]
+    erow[0:TAPS] = grad_a
     one = spread(back[0], back[1])
     two = spread(back[2], back[3])
     erow[16:24] = jnp.concatenate(one + two, axis=0)
-    norm_a = rstd_a * (sums[0:16] - qq[0:16, 32:33] * mean_a)
-    norm_b = rstd_b * (sums[16:32] - qq[16:32, 33:34] * mean_b)
-    per = spread(norm_a, norm_b)
-    for u in range(utts):
-        erow[24 + u * TAPS : 24 + (u + 1) * TAPS] = per[u][:TAPS]
-    for u, w in enumerate(spread(qq[32:33], qq[33:34])):
+    norm_a = rstd_a * (pre_a - w_a * mean_a)
+    norm_b = rstd_b * (pre_b - w_b * mean_b)
+    for u, value in enumerate(spread(norm_a, norm_b)):
+        erow[24 + u * TAPS : 24 + (u + 1) * TAPS] = value
+    erow[10:16] = jnp.zeros((6, channels), F32)
+    for u, w in enumerate(spread(w_rows[0:1], w_rows[1:2])):
         erow[10 + u : 11 + u, 0:128] = w
     high = erow.shape[0] // 8
     for c in range(blocks):
@@ -338,35 +388,37 @@
         me, orders[3], ex, ex_in, ex_out, blocks * high, send_sems.at[3], recv_sems.at[3]
     )
     extra.start()
-    for _ in range(2 * bits - 1):
+    for _ in range(2 * bits):
         for part in parts:
-            part.step()
+            if part.at < 2 * bits:
+                part.step()
         extra.step()
-    extra.finish()
-    for t in range(3):
-        for c in range(blocks):
-            grad2_ref[t * channels : (t + 1) * channels, c * 128 : (c + 1) * 128] = (
-                outb[t * size + c * tall : t * size + (c + 1) * tall].reshape(channels, 128) * factor
-            )
     for c in range(blocks):
         erow[:, c * 128 : (c + 1) * 128] = ex_out[c * high : (c + 1) * high].reshape(8 * high, 128)
     weights, scales = [], []
     result = erow[0:TAPS]
     for u in range(utts):
         weights.append(erow[10 + u : 11 + u, 0:128])
-        scales.append(rstds[u] * (erow[16 + u : 17 + u] / inverse[u]))
-        result = result - rstds[u] * (erow[16 + utts + u : 17 + utts + u] / inverse[u]) * (
+        scales.append(rstds[u] * (erow[16 + u : 17 + u] / counts[u]))
+        result = result - rstds[u] * (erow[16 + utts + u : 17 + utts + u] / counts[u]) * (
             erow[24 + u * TAPS : 24 + (u + 1) * TAPS]
         )
     pad = [jnp.zeros((8 - utts, 128), F32)], [jnp.zeros((8 - utts, channels), F32)]
     plain = dot_tn(
         jnp.concatenate(weights + pad[0], axis=0), jnp.concatenate(scales + pad[1], axis=0), HIGH
     )
-    grad1_ref[...] = (result - plain[0:TAPS] - plain[16 : 16 + TAPS]) * factor
+    grad1_ref[...] = (result - plain[0:TAPS] - plain[32 : 32 + TAPS]) * factor
+    halo.wait_send()
     for copy in stat_copies:
         copy.wait_send()
     for part in parts + [extra]:
         part.drain()
+
+
+def finish(factor, feat_in, grad1_in, tiled_ref, feat_ref, grad1_ref, grad2_ref):
+    feat_ref[...] = feat_in[...]
+    grad1_ref[...] = grad1_in[...]
+    grad2_ref[...] = tiled_ref[...].reshape(grad2_ref.shape) * factor
 
 
 def on_device(waveform, lengths, conv_first, conv_second, cotangent):
@@ -376,32 +428,27 @@
     channels = conv_second.shape[1]
     utts = lengths.shape[1]
     assert 24 + utts * TAPS <= 64 and utts == 4 and samples.shape[0] < MIN_UNITS * 640
-    ahead = lax.ppermute(samples[:TAPS], "seq", [(i, i - 1) for i in range(1, n)])
-    table = jnp.concatenate([samples, ahead]).reshape(rows + 1, TAPS)
-    middle = jnp.concatenate([table[:-1, 5:], table[1:, :5]], axis=1)
-    taps = jnp.concatenate([table[:-1], middle, table[1:]], axis=0)
     count = 3 * rows
-    gap = jnp.zeros((count, 6), F32)
-    taps = jnp.concatenate(
-        [taps, gap, taps, gap, jnp.ones((count, 2), F32), jnp.zeros((count, 94), F32)], axis=1
-    )
-    first = jnp.concatenate([conv_first, jnp.zeros((128 - TAPS, channels), F32)], axis=0)
     factor = float(lax.axis_size("dp") * rows * n) ** (-0.5)
     tiles = 3 * channels // 8 * (channels // 128)
     small = 64 // 8 * (channels // 128)
     bits = n.bit_length() - 1
     vmem = pl.BlockSpec(memory_space=pltpu.VMEM)
-    feats, grad1, grad2 = pl.pallas_call(
+    feats, grad1, tiled = pl.pallas_call(
         functools.partial(kernel, n, factor),
         name="encoder",
         out_shape=(
             jax.ShapeDtypeStruct((rows, channels), jnp.bfloat16),
             jax.ShapeDtypeStruct((TAPS, channels), F32),
-            jax.ShapeDtypeStruct((3 * channels, channels), F32),
+            jax.ShapeDtypeStruct((tiles, 8, 128), F32),
         ),
         in_specs=[pl.BlockSpec(memory_space=pltpu.SMEM)] + [vmem] * 4,
         out_specs=(vmem, vmem, vmem),
         scratch_shapes=[
+            pltpu.VMEM((rows + 8, 128), F32),
+            pltpu.VMEM((8, 128), F32),
+            pltpu.VMEM((rows, 128), F32),
+            pltpu.VMEM((3 * 128, channels), F32),
             pltpu.VMEM((count, channels), F32),
             pltpu.VMEM((count, channels), F32),
             pltpu.VMEM((count, 128), F32),
@@ -409,7 +456,6 @@
             pltpu.VMEM((rows, channels), jnp.bfloat16),
             pltpu.VMEM((8, 2 * utts, channels), F32),
             pltpu.VMEM((max(1, n // 8), 2 * utts, channels), F32),
-            pltpu.VMEM((tiles, 8, 128), F32),
             pltpu.VMEM((tiles, 8, 128), F32),
             pltpu.VMEM((tiles, 8, 128), F32),
             pltpu.VMEM((small, 8, 128), F32),
@@ -420,11 +466,33 @@
             pltpu.SemaphoreType.DMA((4, 2 * bits)),
             pltpu.SemaphoreType.DMA((8 + n // 8,)),
             pltpu.SemaphoreType.DMA((8 + n // 8,)),
+            pltpu.SemaphoreType.DMA((2,)),
         ],
         compiler_params=pltpu.CompilerParams(
             collective_id=0, has_side_effects=True, vmem_limit_bytes=60 * 1024 * 1024
         ),
-    )(lengths, taps, first, conv_second, cotangent[0])
+    )(lengths, waveform.reshape(rows, TAPS), conv_first, conv_second, cotangent[0])
+    cols = channels // 128
+    feats, grad1, grad2 = pl.pallas_call(
+        functools.partial(finish, factor),
+        name="finish",
+        grid=(cols,),
+        out_shape=(
+            jax.ShapeDtypeStruct((rows, channels), jnp.bfloat16),
+            jax.ShapeDtypeStruct((TAPS, channels), F32),
+            jax.ShapeDtypeStruct((3 * channels, channels), F32),
+        ),
+        in_specs=[
+            pl.BlockSpec((rows // cols, channels), lambda i: (i, 0)),
+            pl.BlockSpec((TAPS, 128), lambda i: (0, i)),
+            pl.BlockSpec((3, 1, channels // 8, 8, 128), lambda i: (0, i, 0, 0, 0)),
+        ],
+        out_specs=(
+            pl.BlockSpec((rows // cols, channels), lambda i: (i, 0)),
+            pl.BlockSpec((TAPS, 128), lambda i: (0, i)),
+            pl.BlockSpec((3 * channels, 128), lambda i: (0, i)),
+        ),
+    )(feats, grad1, tiled.reshape(3, cols, channels // 8, 8, 128))
     if lax.axis_size("dp") > 1:
         grad1, grad2 = lax.psum((grad1, grad2), "dp")
     return (feats[None], grad1, grad2)

time: 100 us -> 92.4 us (0.924)
  local copies, waits for them, and re-layouts: 13.1 us -> 1.43 us
  Pallas kernels: 80.6 us -> 88.6 us
  starting transfers between devices: 1.95 us -> 0 us
  other arithmetic: 3.1 us -> 1.42 us
    unnamed x4 -> x1, local copies, waits for them, and re-layouts: 7.61 us -> 0.51 us
    pallas_call x0 -> x1, Pallas kernels: none -> 4.52 us  [on_device(): pl.pallas_call(functools.partial(finish, factor), name='finish', grid=(co...]
    concatenate x2 -> x0, local copies, waits for them, and re-layouts: 3.93 us -> none  [the longest x1 2.44 us: on_device(): jnp.concatenate([taps, gap, taps, gap, jnp.ones((count, 2), F32), jnp.zer...]
    pallas_call x1, Pallas kernels: 80.6 us -> 84.1 us  [on_device(): pl.pallas_call(functools.partial(kernel, n, factor), name='encoder', out_...]
    ppermute x1 -> x0, starting transfers between devices: 1.95 us -> none  [on_device(): lax.ppermute(samples[:TAPS], 'seq', [(i, i - 1) for i in range(1, n)])]
    concatenate x3 -> x0, other arithmetic: 1.67 us -> none  [the longest x2 1.54 us: on_device(): table = jnp.concatenate([samples, ahead]).reshape(rows + 1, TAPS)]
    slice x4 -> x0, local copies, waits for them, and re-layouts: 1.22 us -> none  [the longest x1 0.66 us: on_device(): samples[:TAPS]]
  transfers between devices with their start and end apart: 1 -> 0, of which waited for: 1 -> 0; matrix products, arithmetic and copies ran while one was open for 4% -> 0% of each run, Pallas kernels for 0% -> 0%
where the time goes in v2:
time: 92.4 us; the launch traced here: 92.1 us
  Pallas kernels  88.6 us (96%)
  local copies, waits for them, and re-layouts  1.43 us (2%)
  other arithmetic  1.42 us (2%)
    pallas_call x1, Pallas kernels, on_device(): pl.pallas_call(functools.partial(kernel, n, factor), name='encoder', out_...  84.1 us
    pallas_call x1, Pallas kernels, on_device(): pl.pallas_call(functools.partial(finish, factor), name='finish', grid=(co...  4.52 us

profile of v2, /device:TPU:1, one launch (start us, length us, event | category | flops | bytes accessed | tf_op | source)
XLA Modules:
  0.0 92.1 jit_solution(16148918539258640948)
XLA Ops:
  0.6 0.5 broadcast.3
  1.1 1.4 %reduce.3 = f32[5120]{0:T(1024)S(1)} reduce(f32[1,5120]{1,0:T(1,128)} %param.5, f32[]{:T(128)} %broadcast.3), dimensions={0}, to_apply=%param.5.reduce_sub_computation.3 | reduce | bytes 40964 | tf_op args[0]
  2.6 0.9 reshape.12.wave_ref
  3.5 84.1 %encoder.1 = (bf16[512,512]{1,0:T(8,128)(2,1)}, f32[10,512]{1,0:T(8,128)}, f32[768,8,128]{2,1,0:T(8,128)}) custom-call(s32[1,4]{1,0:T(1,128)} %lengths_ref.1, f32[512,10]{1,0:T(8,128)} %reshape.12.wave_ref, f32[10,512]{1,0:T(8,128)} %conv_ref.1, bf16[1536,512]{1,0:T(8,128)(2,1)} %second_ref.1, bf16[512,512]{1,0:T(8,128)(2,1)} %bitcast.4), custom_call_target="tpu_custom_call" | custom-call | tf_op jit(solution)/shard_map/encoder/pallas_call | solution.py:437
  87.6 4.5 %finish.1 = (bf16[512,512]{1,0:T(8,128)(2,1)}, f32[10,512]{1,0:T(8,128)}, f32[1536,512]{1,0:T(8,128)}) custom-call(bf16[512,512]{1,0:T(8,128)(2,1)} %get-tuple-element.9.feat_in, f32[10,512]{1,0:T(8,128)} %get-tuple-element.10.grad1_in, f32[3,4,64,8,128]{4,3,2,1,0:T(8,128)} %bitcast.3), custom_call_target="tpu_custom_call" | custom-call | tf_op jit(solution)/shard_map/finish/pallas_call | solution.py:476

commit v3 on v2

--- a/solution.py
+++ b/solution.py
@@ -27,8 +27,13 @@
 
 def stage_orders(bits):
     if bits != 5:
-        return [list(range(bits))] * 4
-    return [[0, 1, 2, 3, 4], [0, 2, 3, 1, 4], [0, 3, 1, 2, 4], [0, 1, 2, 3, 4]]
+        return [list(range(bits))] * 7
+    return [
+        [0, 1, 2, 3, 4], [0, 1, 3, 2, 4],
+        [0, 2, 3, 1, 4], [0, 2, 1, 3, 4],
+        [0, 3, 1, 2, 4], [0, 3, 2, 1, 4],
+        [0, 1, 2, 3, 4],
+    ]
 
 
 class Part:
@@ -332,17 +337,19 @@
     size = blocks * tall
     parts = []
     for t in range(3):
-        part = Part(
-            me, orders[t], buf.at[pl.ds(t * size, size)], inbox.at[pl.ds(t * size, size)],
-            outb.at[pl.ds(t * size, size)], size, send_sems.at[t], recv_sems.at[t],
-        )
         grad = dot_tn(x_ref[t * rows : (t + 1) * rows], sd_ref[...])
         for c in range(blocks):
             buf[t * size + c * tall : t * size + (c + 1) * tall] = grad[
                 :, c * 128 : (c + 1) * 128
             ].reshape(tall, 8, 128)
-        part.start()
-        parts.append(part)
+        for k in (2 * t, 2 * t + 1):
+            at = pl.ds(k * (size // 2), size // 2)
+            part = Part(
+                me, orders[k], buf.at[at], inbox.at[at], outb.at[at], size // 2,
+                send_sems.at[k], recv_sems.at[k],
+            )
+            part.start()
+            parts.append(part)
 
     back = (zero_row, zero_row, zero_row, zero_row)
     for t in range(3):
@@ -385,7 +392,7 @@
     for c in range(blocks):
         ex[c * high : (c + 1) * high] = erow[:, c * 128 : (c + 1) * 128].reshape(high, 8, 128)
     extra = Part(
-        me, orders[3], ex, ex_in, ex_out, blocks * high, send_sems.at[3], recv_sems.at[3]
+        me, orders[6], ex, ex_in, ex_out, blocks * high, send_sems.at[6], recv_sems.at[6]
     )
     extra.start()
     for _ in range(2 * bits):
@@ -462,8 +469,8 @@
             pltpu.VMEM((small, 8, 128), F32),
             pltpu.VMEM((small, 8, 128), F32),
             pltpu.VMEM((64, channels), F32),
-            pltpu.SemaphoreType.DMA((4, 2 * bits)),
-            pltpu.SemaphoreType.DMA((4, 2 * bits)),
+            pltpu.SemaphoreType.DMA((7, 2 * bits)),
+            pltpu.SemaphoreType.DMA((7, 2 * bits)),
             pltpu.SemaphoreType.DMA((8 + n // 8,)),
             pltpu.SemaphoreType.DMA((8 + n // 8,)),
             pltpu.SemaphoreType.DMA((2,)),

time: 92.4 us -> 90.1 us (0.975)
  Pallas kernels: 88.6 us -> 86.3 us
    pallas_call x1, Pallas kernels: 84.1 us -> 81.8 us  [on_device(): pl.pallas_call(functools.partial(kernel, n, factor), name='encoder', out_...]
where the time goes in v3:
time: 90.1 us; the launch traced here: 89.8 us
  Pallas kernels  86.3 us (96%)
  local copies, waits for them, and re-layouts  1.43 us (2%)
  other arithmetic  1.42 us (2%)
    pallas_call x1, Pallas kernels, on_device(): pl.pallas_call(functools.partial(kernel, n, factor), name='encoder', out_...  81.8 us
    pallas_call x1, Pallas kernels, on_device(): pl.pallas_call(functools.partial(finish, factor), name='finish', grid=(co...  4.52 us

profile of v3, /device:TPU:1, one launch (start us, length us, event | category | flops | bytes accessed | tf_op | source)
XLA Modules:
  0.0 89.8 jit_solution(3647060079297151572)
XLA Ops:
  0.6 0.5 broadcast.3
  1.1 1.4 %reduce.3 = f32[5120]{0:T(1024)S(1)} reduce(f32[1,5120]{1,0:T(1,128)} %param.5, f32[]{:T(128)} %broadcast.3), dimensions={0}, to_apply=%param.5.reduce_sub_computation.3 | reduce | bytes 40964 | tf_op args[0]
  2.6 0.9 %reshape.12.wave_ref = f32[512,10]{1,0:T(8,128)} reshape(f32[5120]{0:T(1024)S(1)} %reduce.3) | data formatting | bytes 40960 | tf_op jit(solution)/shard_map/reshape | solution.py:481
  3.5 81.8 %encoder.1 = (bf16[512,512]{1,0:T(8,128)(2,1)}, f32[10,512]{1,0:T(8,128)}, f32[768,8,128]{2,1,0:T(8,128)}) custom-call(s32[1,4]{1,0:T(1,128)} %lengths_ref.1, f32[512,10]{1,0:T(8,128)} %reshape.12.wave_ref, f32[10,512]{1,0:T(8,128)} %conv_ref.1, bf16[1536,512]{1,0:T(8,128)(2,1)} %second_ref.1, bf16[512,512]{1,0:T(8,128)(2,1)} %bitcast.4), custom_call_target="tpu_custom_call" | custom-call | tf_op jit(solution)/shard_map/encoder/pallas_call | solution.py:444
  85.3 4.5 %finish.1 = (bf16[512,512]{1,0:T(8,128)(2,1)}, f32[10,512]{1,0:T(8,128)}, f32[1536,512]{1,0:T(8,128)}) custom-call(bf16[512,512]{1,0:T(8,128)(2,1)} %get-tuple-element.9.feat_in, f32[10,512]{1,0:T(8,128)} %get-tuple-element.10.grad1_in, f32[3,4,64,8,128]{4,3,2,1,0:T(8,128)} %bitcast.3), custom_call_target="tpu_custom_call" | custom-call | tf_op jit(solution)/shard_map/finish/pallas_call | solution.py:483

commit v4 on v3

--- a/solution.py
+++ b/solution.py
@@ -145,7 +145,7 @@
         barrier, inc=1, device_id={"seq": lax.rem(me + 1, n)}, device_id_type=MESH
     )
     tab_ref[...] = jnp.zeros_like(tab_ref)
-    tab_ref[0:rows, 0:TAPS] = wave_ref[...]
+    tab_ref[0 : rows + 8, 0:TAPS] = wave_ref[...]
     first_ref[...] = jnp.zeros_like(first_ref)
     for t in range(3):
         first_ref[t * 128 + 5 * t : t * 128 + 5 * t + TAPS] = conv_ref[...]
@@ -350,6 +350,9 @@
             )
             part.start()
             parts.append(part)
+        for part in parts[: 2 * t]:
+            if part.at == 0:
+                part.step()
 
     back = (zero_row, zero_row, zero_row, zero_row)
     for t in range(3):
@@ -369,8 +372,9 @@
             return tuple(c + jnp.sum(a, axis=0, keepdims=True) for c, a in zip(carry, add))
 
         back = lax.fori_loop(0, rows // BLOCK, back_block, back)
-        for part in parts:
-            part.step()
+        if t < 2:
+            for part in parts[4 - 4 * t :]:
+                part.step()
     acc = [by_tap(slope_ref, t) for t in range(3)]
 
     grad_a = jnp.zeros((TAPS, channels), F32)
@@ -395,11 +399,14 @@
         me, orders[6], ex, ex_in, ex_out, blocks * high, send_sems.at[6], recv_sems.at[6]
     )
     extra.start()
-    for _ in range(2 * bits):
-        for part in parts:
+    for turn in range(2 * bits):
+        for i, part in enumerate(parts):
             if part.at < 2 * bits:
                 part.step()
-        extra.step()
+            if i == len(parts) // 2 - 1 and turn < 4 and extra.at < 2 * bits:
+                extra.step()
+        if extra.at < 2 * bits:
+            extra.step()
     for c in range(blocks):
         erow[:, c * 128 : (c + 1) * 128] = ex_out[c * high : (c + 1) * high].reshape(8 * high, 128)
     weights, scales = [], []
@@ -436,6 +443,7 @@
     utts = lengths.shape[1]
     assert 24 + utts * TAPS <= 64 and utts == 4 and samples.shape[0] < MIN_UNITS * 640
     count = 3 * rows
+    table = jnp.pad(waveform[0], (0, 8 * TAPS)).reshape(rows + 8, TAPS)
     factor = float(lax.axis_size("dp") * rows * n) ** (-0.5)
     tiles = 3 * channels // 8 * (channels // 128)
     small = 64 // 8 * (channels // 128)
@@ -478,7 +486,7 @@
         compiler_params=pltpu.CompilerParams(
             collective_id=0, has_side_effects=True, vmem_limit_bytes=60 * 1024 * 1024
         ),
-    )(lengths, waveform.reshape(rows, TAPS), conv_first, conv_second, cotangent[0])
+    )(lengths, table, conv_first, conv_second, cotangent[0])
     cols = channels // 128
     feats, grad1, grad2 = pl.pallas_call(
         functools.partial(finish, factor),

time: 90.1 us -> 88 us (0.977)
  other arithmetic: 1.42 us -> 0 us
    unnamed x1 -> x0, other arithmetic: 1.42 us -> none
    pallas_call x1, Pallas kernels: 81.8 us -> 80.8 us  [on_device(): pl.pallas_call(functools.partial(kernel, n, factor), name='encoder', out_...]
where the time goes in v4:
time: 88 us; the launch traced here: 87.7 us
  Pallas kernels  85.4 us (97%)
  local copies, waits for them, and re-layouts  1.68 us (2%)
    pallas_call x1, Pallas kernels, on_device(): pl.pallas_call(functools.partial(kernel, n, factor), name='encoder', out_...  80.8 us
    pallas_call x1, Pallas kernels, on_device(): pl.pallas_call(functools.partial(finish, factor), name='finish', grid=(co...  4.52 us

profile of v4, /device:TPU:1, one launch (start us, length us, event | category | flops | bytes accessed | tf_op | source)
XLA Modules:
  0.0 87.7 jit_solution(8441089613025997968)
XLA Ops:
  0.6 0.7 pad.4
  1.4 0.9 %reshape.12.wave_ref = f32[520,10]{1,0:T(8,128)} reshape(f32[5200]{0:T(1024)S(1)} %pad.4) | data formatting | bytes 41600 | tf_op jit(solution)/shard_map/reshape | solution.py:446
  2.3 80.8 %encoder.1 = (bf16[512,512]{1,0:T(8,128)(2,1)}, f32[10,512]{1,0:T(8,128)}, f32[768,8,128]{2,1,0:T(8,128)}) custom-call(s32[1,4]{1,0:T(1,128)} %lengths_ref.1, f32[520,10]{1,0:T(8,128)} %reshape.12.wave_ref, f32[10,512]{1,0:T(8,128)} %conv_ref.1, bf16[1536,512]{1,0:T(8,128)(2,1)} %second_ref.1, bf16[512,512]{1,0:T(8,128)(2,1)} %bitcast.5), custom_call_target="tpu_custom_call" | custom-call | tf_op jit(solution)/shard_map/encoder/pallas_call | solution.py:452
  83.2 4.5 %finish.1 = (bf16[512,512]{1,0:T(8,128)(2,1)}, f32[10,512]{1,0:T(8,128)}, f32[1536,512]{1,0:T(8,128)}) custom-call(bf16[512,512]{1,0:T(8,128)(2,1)} %get-tuple-element.9.feat_in, f32[10,512]{1,0:T(8,128)} %get-tuple-element.10.grad1_in, f32[3,4,64,8,128]{4,3,2,1,0:T(8,128)} %bitcast.4), custom_call_target="tpu_custom_call" | custom-call | tf_op jit(solution)/shard_map/finish/pallas_call | solution.py:491
